TPU v7x, 256 devices: a whole 4x4x8 slice. The times are simulated.
256 devices in a mesh: pass: 64 (over z, y, core), voc: 4 (over x).
Axes of the slice: x: 4, y: 4, z: 8, core: 2. Of those that a mesh axis runs over, the one named last changes fastest.
Arguments:
- hidden: bfloat16 [2048, 16, 768], P('pass'), may hold values from -6 to 6
- positions: int32 [2048, 8], P('pass'), may hold values from 0 to 15
- passage_weight: float32 [2048], P('pass'), may hold values from 0.4 to 2.5
- passage_counts: int32 [128], replicated, may hold values from 1 to 24, 2048 in all
- passage_slot: int32 [2048], replicated, may hold values from 0 to 2047, each once
- head_weight: bfloat16 [768, 30720], P(None, 'voc'), may hold values from -0.21875 to 0.21875
- head_bias: float32 [30720], P('voc'), may hold values from -5 to 5
- queries: bfloat16 [128, 30720], P('pass', 'voc'), may hold values from -1 to 1
Outputs:
- scores: float32 [128, 128], P('pass')
- hidden_grad: bfloat16 [2048, 16, 768], P('pass')
Inputs may be any that keep to these rules, and one draw needn't show every extreme that they name: `passage_slot`: each slot holds exactly one passage.
All inputs are finite; a program needn't handle non-finite values.
Results may differ from a plain program's by a relative error of at most 0.015.
Values may be sent and summed in bfloat16 or wider, within the bound.
A program may use at most 64 MiB of HBM per device.

v0:
```python
import jax
import jax.numpy as jnp
from jax import lax
from jax.sharding import PartitionSpec as P

HIGH = lax.Precision.HIGHEST


def sent_to_all(array, axis):
    size = lax.axis_size(axis)
    return lax.all_to_all(
        jnp.broadcast_to(array[None], (size, *array.shape)), axis, 0, 0, tiled=True
    )


def over_copies(array, axis):
    return sent_to_all(array, axis).sum(axis=0)


def in_order(tiles, dim):
    tiles = jnp.moveaxis(tiles, 0, dim)
    shape = tiles.shape
    return tiles.reshape(*shape[:dim], shape[dim] * shape[dim + 1], *shape[dim + 2 :])


def gathered_copies(array, axis, dim):
    tiles = sent_to_all(array, axis)
    return in_order(tiles, dim)


def in_blocks(array, dim, size):
    before, after = (array.shape[:dim], array.shape[dim + 1 :])
    return jnp.moveaxis(array.reshape(*before, size, -1, *after), dim, 0)


def summed_on_arrival(array, axis, dim):
    size = lax.axis_size(axis)
    tiles = lax.all_to_all(in_blocks(array, dim, size), axis, 0, 0, tiled=True)
    return jnp.sum(tiles, axis=0)


def of_everyone(array, axis):
    return sent_to_all(array, axis).astype(jnp.float32).sum(axis=0)


def vocab_total(partial_value):
    return over_copies(partial_value, "voc")


def score_gradient(scores, owned, doc_total):
    query_first = lax.axis_index("pass") * owned
    rows = query_first + jnp.arange(owned, dtype=jnp.int32)
    target = (jnp.arange(doc_total, dtype=jnp.int32)[None, :] == rows[:, None]).astype(jnp.float32)
    prob = jax.nn.softmax(scores, axis=1)
    return (prob - target) / doc_total


def on_device(
    hidden, positions, passage_weight, passage_counts, passage_slot, head_weight, head_bias, queries
):
    count = hidden.shape[0]
    seq_len = hidden.shape[1]
    width = hidden.shape[2]
    picks = positions.shape[1]
    total = passage_slot.shape[0]
    doc_total = passage_counts.shape[0]
    owned = queries.shape[0]
    vocab_local = head_weight.shape[1]
    ends = jnp.cumsum(passage_counts)
    order = jnp.arange(total, dtype=jnp.int32)
    doc_order = jnp.sum((ends[None, :] <= order[:, None]).astype(jnp.int32), axis=1)
    local_slot = lax.axis_index("pass") * count + jnp.arange(count, dtype=jnp.int32)
    matched = passage_slot[None, :] == local_slot[:, None]
    doc_local = jnp.sum(jnp.where(matched, doc_order[None, :], 0), axis=1)
    mixing = jnp.where(
        doc_local[None, :] == jnp.arange(doc_total, dtype=jnp.int32)[:, None],
        passage_weight[None, :],
        jnp.float32(0.0),
    )
    picked = jax.vmap(lambda h, p: h[p])(hidden, positions).reshape(-1, width)
    logits = jnp.dot(picked, head_weight, preferred_element_type=jnp.float32) + head_bias
    active = jnp.log1p(jnp.maximum(logits, 0.0))
    rep = active.reshape(count, picks, vocab_local).sum(axis=1).astype(jnp.bfloat16)
    all_queries = gathered_copies(queries, "pass", 0)
    paired = lax.dot_general(
        all_queries, rep, (((1,), (1,)), ((), ())), preferred_element_type=jnp.float32
    )
    parts = lax.dot_general(paired, mixing, (((1,), (1,)), ((), ())), precision=HIGH)
    scores = vocab_total(summed_on_arrival(parts, "pass", 0))
    dscore = score_gradient(scores, owned, doc_total)
    all_dscore = gathered_copies(dscore, "pass", 0)
    per_query = lax.dot_general(mixing, all_dscore, (((0,), (1,)), ((), ())), precision=HIGH)
    drep = jnp.dot(per_query, all_queries.astype(jnp.float32), precision=HIGH)
    shaped = logits.reshape(count, picks, vocab_local)
    growth = 1.0 + jnp.maximum(shaped, 0.0)
    dlogits = jnp.where(shaped > 0, drep[:, None, :] / growth, jnp.float32(0.0)).astype(
        jnp.bfloat16
    )
    token_part = lax.dot_general(
        dlogits.reshape(-1, vocab_local),
        head_weight,
        (((1,), (1,)), ((), ())),
        preferred_element_type=jnp.float32,
    )
    dpicked = of_everyone(token_part.astype(jnp.bfloat16), "voc").astype(jnp.float32)
    onehot = (positions[:, :, None] == jnp.arange(seq_len, dtype=jnp.int32)[None, None, :]).astype(
        jnp.float32
    )
    hidden_grad = jnp.einsum(
        "bps,bpd->bsd", onehot, dpicked.reshape(count, picks, width), precision=HIGH
    )
    return (scores, hidden_grad.astype(jnp.bfloat16))


def solution(mesh):
    placed = (
        P("pass", None, None),
        P("pass", None),
        P("pass"),
        P(),
        P(),
        P(None, "voc"),
        P("voc"),
        P("pass", "voc"),
    )
    return jax.shard_map(
        on_device,
        mesh=mesh,
        in_specs=placed,
        out_specs=(P("pass", None), P("pass", None, None)),
        check_vma=False,
    )
```

profile of v0, /device:TPU:1, one launch (start us, length us, event | category | flops | bytes accessed | tf_op | source)
XLA Modules:
  0.0 151.9 jit_solution(6355383206969645016)
XLA Ops:
  0.6 0.0 copy-start
  0.6 0.0 copy-start.3
  0.7 0.0 copy-start.5
  0.7 3.1 %broadcast_in_dim.36 = bf16[64,2,7680]{2,1,0:T(2,128)(2,1)} broadcast(bf16[2,7680]{1,0:T(2,128)(2,1)} %param.15), dimensions={1,2} | broadcast | bytes 1996800 | tf_op jit(solution)/shard_map/broadcast_in_dim | solution.py:12
  3.8 13.3 %all-to-all-start = ((bf16[64,2,7680]{2,1,0:T(2,128)(2,1)}), bf16[64,2,7680]{2,1,0:T(2,128)(2,1)}, u32[]{:S(2)}, u32[]{:S(2)}) async-start(bf16[64,2,7680]{2,1,0:T(2,128)(2,1)} %broadcast_in_dim.36), calls=%async_computation | async-start | bytes 3932160 | tf_op jit(solution)/shard_map/all_to_all | solution.py:11
  17.1 0.7 fusion.24
  17.8 0.1 copy.18
  17.9 0.1 reshape.124
  18.0 0.8 copy.19
  18.7 0.2 reduce-window.8
  18.9 0.1 reduce
  19.0 0.0 copy-done
  19.0 2.4 %gather_fusion = bf16[256,768]{1,0:T(8,128)(2,1)S(1)} fusion(bf16[32,16,768]{2,1,0:T(8,128)(2,1)S(1)} %copy-done, s32[256]{0:T(256)S(1)} %reshape.124), kind=kCustom, calls=%fused_computation | custom fusion | bytes 788480 | tf_op jit(solution)/shard_map/vmap()/gather | solution.py:80
  21.5 0.3 convert_reduce_fusion.1
  21.8 0.0 copy-done.3
  21.8 0.2 select_reduce_fusion
  22.0 0.0 copy-done.5
  22.0 0.0 copy-start.4
  22.0 14.1 %bitcast_reduce_fusion = (bf16[32,7680]{1,0:T(8,128)(2,1)S(1)}, f32[256,7680]{1,0:T(8,128)}) fusion(f32[7680]{0:T(1024)S(1)} %copy-done.5, bf16[256,768]{1,0:T(8,128)(2,1)S(1)} %gather_fusion, bf16[768,7680]{1,0:T(8,128)(2,1)} %param.13), kind=kOutput, calls=%fused_computation.5 | convolution fusion | flops 3025551360 | bytes 20576256 | tf_op jit(solution)/shard_map/dot_general | solution.py:81
  36.1 27.9 %all-to-all-done = bf16[64,2,7680]{2,1,0:T(2,128)(2,1)} async-done(((bf16[64,2,7680]{2,1,0:T(2,128)(2,1)}), bf16[64,2,7680]{2,1,0:T(2,128)(2,1)}, u32[]{:S(2)}, u32[]{:S(2)}) %all-to-all-start) | async-done | bytes 1966112 | tf_op jit(solution)/shard_map/all_to_all | solution.py:11
  64.1 4.2 %reshape.118 = bf16[128,7680]{1,0:T(8,128)(2,1)S(1)} reshape(bf16[64,2,7680]{2,1,0:T(2,128)(2,1)} %all-to-all-done) | data formatting | bytes 3932160 | tf_op jit(solution)/shard_map/reshape | solution.py:23
  68.3 0.7 fusion.32
  69.0 0.0 copy-done.4
  69.0 1.0 fusion.12
  70.0 6.8 %all-to-all-start.1 = ((f32[64,2,128]{2,1,0:T(2,128)}), f32[64,2,128]{2,1,0:T(2,128)S(1)}, u32[]{:S(2)}, u32[]{:S(2)}) async-start(f32[64,2,128]{2,1,0:T(2,128)} %bitcast.3), calls=%async_computation.1 | async-start | bytes 131072 | tf_op jit(solution)/shard_map/all_to_all | solution.py:38
  76.8 10.1 %all-to-all-done.1 = f32[64,2,128]{2,1,0:T(2,128)S(1)} async-done(((f32[64,2,128]{2,1,0:T(2,128)}), f32[64,2,128]{2,1,0:T(2,128)S(1)}, u32[]{:S(2)}, u32[]{:S(2)}) %all-to-all-start.1) | async-done | bytes 65568 | tf_op jit(solution)/shard_map/all_to_all | solution.py:38
  86.9 0.1 reduce_sum.66
  86.9 0.6 broadcast_in_dim.41
  87.5 4.0 %all-to-all-start.2 = ((f32[4,2,128]{2,1,0:T(2,128)}), f32[4,2,128]{2,1,0:T(2,128)S(1)}, u32[]{:S(2)}, u32[]{:S(2)}) async-start(f32[4,2,128]{2,1,0:T(2,128)} %broadcast_in_dim.41), calls=%async_computation.2 | async-start | bytes 8192 | tf_op jit(solution)/shard_map/all_to_all | solution.py:11
  91.6 4.1 %all-to-all-done.2 = f32[4,2,128]{2,1,0:T(2,128)S(1)} async-done(((f32[4,2,128]{2,1,0:T(2,128)}), f32[4,2,128]{2,1,0:T(2,128)S(1)}, u32[]{:S(2)}, u32[]{:S(2)}) %all-to-all-start.2) | async-done | bytes 4128 | tf_op jit(solution)/shard_map/all_to_all | solution.py:11
  95.7 0.0 copy-start.2
  95.7 0.1 reduce_max.9
  95.8 0.2 fusion.26
  96.0 0.1 fusion.25
  96.1 15.3 %all_to_all.25 = f32[64,2,128]{2,1,0:T(2,128)S(1)} all-to-all(f32[64,2,128]{2,1,0:T(2,128)S(1)} %broadcast_in_dim.42), channel_id=1, replica_groups=mesh['pass'=64,'voc'=4] {'pass'}, dimensions={0} | all-to-all | bytes 131072 | tf_op jit(solution)/shard_map/all_to_all | solution.py:11
  111.5 0.2 fusion.10
  111.7 2.0 %fusion.31 = f32[32,7680]{1,0:T(8,128)} fusion(f32[32,128]{1,0:T(8,128)S(1)} %fusion.10, bf16[128,7680]{1,0:T(8,128)(2,1)S(1)} %reshape.118), kind=kOutput, calls=%fused_computation.45 | convolution fusion | flops 377487360 | bytes 2965504 | tf_op jit(solution)/shard_map/dot_general | solution.py:93
  113.7 0.0 copy-start.1
  113.7 10.8 %fusion.4 = bf16[256,768]{1,0:T(8,128)(2,1)S(1)} fusion(bf16[768,7680]{1,0:T(8,128)(2,1)} %param.13, f32[256,7680]{1,0:T(8,128)} %get-tuple-element.3, f32[32,7680]{1,0:T(8,128)} %fusion.31), kind=kOutput, calls=%fused_computation.9 | convolution fusion | flops 3031891968 | bytes 21037056 | tf_op jit(solution)/shard_map/dot_general | solution.py:99
  124.5 0.0 copy-done.2
  124.5 1.3 broadcast_in_dim.43
  125.7 3.6 %all-to-all-start.4 = ((bf16[4,256,768]{2,1,0:T(8,128)(2,1)}), bf16[4,256,768]{2,1,0:T(8,128)(2,1)S(1)}, u32[]{:S(2)}, u32[]{:S(2)}) async-start(bf16[4,256,768]{2,1,0:T(8,128)(2,1)} %broadcast_in_dim.43), calls=%async_computation.4 | async-start | bytes 3145728 | tf_op jit(solution)/shard_map/all_to_all | solution.py:11
  129.3 0.0 copy-done.1
  129.3 0.1 copy.21
  129.4 20.3 %all-to-all-done.4 = bf16[4,256,768]{2,1,0:T(8,128)(2,1)S(1)} async-done(((bf16[4,256,768]{2,1,0:T(8,128)(2,1)}), bf16[4,256,768]{2,1,0:T(8,128)(2,1)S(1)}, u32[]{:S(2)}, u32[]{:S(2)}) %all-to-all-start.4) | async-done | bytes 1572896 | tf_op jit(solution)/shard_map/all_to_all | solution.py:11
  149.7 0.2 convert_reduce_fusion
  149.9 2.0 %convolution_convert_fusion = bf16[32,16,768]{2,1,0:T(8,128)(2,1)} fusion(f32[256,768]{1,0:T(8,128)S(1)} %convert_reduce_fusion, s32[32,8]{1,0:T(8,128)S(1)} %copy.21), kind=kOutput, calls=%fused_computation.8 | convolution fusion | flops 38146048 | bytes 1573888 | tf_op jit(solution)/shard_map/bps,bpd->bsd/dot_general | solution.py:109
  (4 shorter events, 0.0 us)
Async XLA Ops:
  0.6 18.4 %copy-start = (bf16[32,16,768]{2,1,0:T(8,128)(2,1)S(1)}, bf16[32,16,768]{2,1,0:T(8,128)(2,1)}, u32[]{:S(2)}) copy-start(bf16[32,16,768]{2,1,0:T(8,128)(2,1)} %param.8) | copy-start | bytes 2359300
  0.6 21.2 %copy-start.3 = (s32[2048]{0:T(1024)S(1)}, s32[2048]{0:T(1024)}, u32[]{:S(2)}) copy-start(s32[2048]{0:T(1024)} %param.12) | copy-start | bytes 24580
  0.7 21.4 %copy-start.5 = (f32[7680]{0:T(1024)S(1)}, f32[7680]{0:T(1024)}, u32[]{:S(2)}) copy-start(f32[7680]{0:T(1024)} %param.14) | copy-start | bytes 92164
  3.8 60.3 %all-to-all-start = ((bf16[64,2,7680]{2,1,0:T(2,128)(2,1)}), bf16[64,2,7680]{2,1,0:T(2,128)(2,1)}, u32[]{:S(2)}, u32[]{:S(2)}) async-start(bf16[64,2,7680]{2,1,0:T(2,128)(2,1)} %broadcast_in_dim.36), calls=%async_computation | async-start | bytes 3932160 | tf_op jit(solution)/shard_map/all_to_all | solution.py:11
  22.0 47.0 %copy-start.4 = (f32[32]{0:T(128)S(1)}, f32[32]{0:T(128)}, u32[]{:S(2)}) copy-start(f32[32]{0:T(128)} %param.10) | copy-start | bytes 388
  70.0 16.9 %all-to-all-start.1 = ((f32[64,2,128]{2,1,0:T(2,128)}), f32[64,2,128]{2,1,0:T(2,128)S(1)}, u32[]{:S(2)}, u32[]{:S(2)}) async-start(f32[64,2,128]{2,1,0:T(2,128)} %bitcast.3), calls=%async_computation.1 | async-start | bytes 131072 | tf_op jit(solution)/shard_map/all_to_all | solution.py:38
  87.5 8.2 %all-to-all-start.2 = ((f32[4,2,128]{2,1,0:T(2,128)}), f32[4,2,128]{2,1,0:T(2,128)S(1)}, u32[]{:S(2)}, u32[]{:S(2)}) async-start(f32[4,2,128]{2,1,0:T(2,128)} %broadcast_in_dim.41), calls=%async_computation.2 | async-start | bytes 8192 | tf_op jit(solution)/shard_map/all_to_all | solution.py:11
  95.7 28.8 %copy-start.2 = (f32[2,128]{1,0:T(2,128)}, f32[2,128]{1,0:T(2,128)S(1)}, u32[]{:S(2)}) copy-start(f32[2,128]{1,0:T(2,128)S(1)} %reduce_sum.67) | copy-start | bytes 3076
  113.7 15.6 %copy-start.1 = (s32[32,8]{0,1:T(8,128)S(1)}, s32[32,8]{0,1:T(8,128)}, u32[]{:S(2)}) copy-start(s32[32,8]{0,1:T(8,128)} %param.9) | copy-start | bytes 3076
  125.7 24.0 %all-to-all-start.4 = ((bf16[4,256,768]{2,1,0:T(8,128)(2,1)}), bf16[4,256,768]{2,1,0:T(8,128)(2,1)S(1)}, u32[]{:S(2)}, u32[]{:S(2)}) async-start(bf16[4,256,768]{2,1,0:T(8,128)(2,1)} %broadcast_in_dim.43), calls=%async_computation.4 | async-start | bytes 3145728 | tf_op jit(solution)/shard_map/all_to_all | solution.py:11
where the time goes:
time: 152 us
  waiting for transfers between devices  62.5 us (41%)
  matrix products  30.7 us (20%)
  starting transfers between devices  27.7 us (18%)
  blocking collectives  15.3 us (10%)
  local copies, waits for them, and re-layouts  12.7 us (8%)
  other arithmetic  2.23 us (1%)
    all_to_all x3, waiting for transfers between devices, sent_to_all(): lax.all_to_all(jnp.broadcast_to(array[None], (size, *array.shape)), axis,...  52.4 us
    all_to_all x3, starting transfers between devices, sent_to_all(): lax.all_to_all(jnp.broadcast_to(array[None], (size, *array.shape)), axis,...  20.9 us
    all_to_all x1, blocking collectives, sent_to_all(): lax.all_to_all(jnp.broadcast_to(array[None], (size, *array.shape)), axis,...  15.3 us
    dot_general x1, matrix products, on_device(): jnp.dot(picked, head_weight, preferred_element_type=jnp.float32) + head_bias  14.1 us
    dot_general x1, matrix products, on_device(): lax.dot_general(dlogits.reshape(-1, vocab_local), head_weight, (((1,), (1...  10.8 us
    all_to_all x1, waiting for transfers between devices, summed_on_arrival(): tiles = lax.all_to_all(in_blocks(array, dim, size), axis, 0, 0, tiled=True)  10.1 us
    all_to_all x1, starting transfers between devices, summed_on_arrival(): tiles = lax.all_to_all(in_blocks(array, dim, size), axis, 0, 0, tiled=True)  6.8 us
    broadcast_in_dim x4, local copies, waits for them, and re-layouts, sent_to_all(): jnp.broadcast_to(array[None], (size, *array.shape))  4.99 us
  transfers between devices with their start and end apart: 4, of which 4 were waited for; matrix products, arithmetic and copies ran while one was open for 13% of the time, Pallas kernels for 0%

commit v1 on v0

v1 whole, which is shorter than its diff:
```python
import functools

import jax
import jax.numpy as jnp
from jax import lax
from jax.experimental import pallas as pl
from jax.experimental.pallas import tpu as pltpu
from jax.sharding import PartitionSpec as P

MESH = pl.DeviceIdType.MESH
CORES = 2
ROWS = 4
QUARTERS = 4
FORWARD = 512
F32 = jnp.float32
BF16 = jnp.bfloat16
NT = (((1,), (1,)), ((), ()))
NN = (((1,), (0,)), ((), ()))
TN = (((0,), (0,)), ((), ()))


def dot(a, b, dims):
    return lax.dot_general(a, b, dims, preferred_element_type=F32)


def halves(a):
    high = a.astype(BF16)
    return high, (a - high.astype(F32)).astype(BF16)


def iota(shape, dim):
    return lax.broadcasted_iota(jnp.int32, shape, dim)


def kernel(
    depth,
    blocks,
    hidden,
    target,
    weights,
    counts,
    slots,
    w_hbm,
    bias,
    q_own,
    scores_out,
    grad_out,
    w,
    inv,
    rep,
    drep,
    qx,
    picked,
    onehot,
    parts,
    box_a,
    box_b,
    box_c,
    scores,
    part_own,
    part_send,
    part_box,
    total,
    w_sem,
    q_sem,
    z_send,
    z_recv,
    y_send,
    y_recv,
    c_send,
    c_recv,
    a_send,
    a_recv,
    b_send,
    b_recv,
    d_send,
    d_recv,
    e_send,
    e_recv,
    r_send,
    r_recv,
    g_send,
    g_recv,
):
    me = lax.axis_index("pass")
    x = lax.axis_index("voc")
    core = lax.rem(me, CORES)
    y = lax.rem(lax.div(me, CORES), ROWS)
    z = lax.div(me, CORES * ROWS)
    group = blocks * CORES
    g = x * CORES + core
    vocab = w.shape[1]
    width = w.shape[0]
    count = rep.shape[0]
    picks = picked.shape[0] // count
    docs_total = counts.shape[1]
    quarter = vocab // QUARTERS
    share = docs_total // group
    steps = vocab // FORWARD
    columns = width // 3
    tokens = picked.shape[0]
    piece_rows = tokens // blocks

    def place(zz, yy, cc):
        return (zz * ROWS + yy) * CORES + cc

    def z_at(k):
        return lax.rem(z + k, depth)

    def y_at(k):
        return lax.rem(y + k, ROWS)

    def x_at(k):
        return lax.rem(x + k, blocks)

    def g_at(k):
        return lax.rem(g + k, group)

    def distance(k):
        odd = lax.rem(k, 2)
        return odd * lax.div(k + 1, 2) + (1 - odd) * lax.rem(depth - lax.div(k, 2), depth)

    other = 1 - core

    def w_copy(step):
        span = pl.ds(pl.multiple_of(step * FORWARD, FORWARD), FORWARD)
        return pltpu.make_async_copy(w_hbm.at[:, span], w.at[:, span], w_sem.at[step])

    q_copy = pltpu.make_async_copy(q_own, qx.at[me], q_sem)
    q_copy.start()

    @pl.loop(0, steps)
    def _(step):
        w_copy(step).start()

    barrier = pltpu.get_barrier_semaphore()
    peers = [(place(z_at(k), y, core), x) for k in range(1, depth)]
    peers += [(place(z, y_at(k), core), x) for k in range(1, ROWS)]
    peers += [(place(z, y, lax.rem(g_at(k), CORES)), lax.div(g_at(k), CORES)) for k in range(1, group)]
    for peer in peers:
        pl.semaphore_signal(barrier, inc=1, device_id=peer, device_id_type=MESH)

    rows = hidden.shape[0]
    hit = (iota((rows, tokens), 0) == target[...]).astype(F32).astype(BF16)
    onehot[...] = hit
    picked[...] = dot(hit, hidden[...], TN).astype(BF16)

    q_copy.wait()
    pl.semaphore_wait(barrier, len(peers))

    def remote(src, dst, send, recv, peer):
        return pltpu.make_async_remote_copy(
            src_ref=src, dst_ref=dst, send_sem=send, recv_sem=recv, device_id=peer, device_id_type=MESH
        )

    def z_copy(k):
        return remote(
            qx.at[me],
            qx.at[me],
            z_send.at[k],
            z_recv.at[k],
            (place(z_at(distance(k)), y, core), x),
        )

    def from_z(k):
        return z_at(depth - distance(k))

    def z_arrival(k):
        spot = qx.at[place(from_z(k), y, core)]
        return remote(spot, spot, z_send.at[k], z_recv.at[k], (place(from_z(k), y, core), x))

    def y_copy(k, j):
        spot = qx.at[place(from_z(k), y, core)]
        return remote(spot, spot, y_send.at[k, j], y_recv.at[k, j], (place(z, y_at(j), core), x))

    def y_arrival(k, j):
        spot = qx.at[place(from_z(k), y_at(ROWS - j), core)]
        return remote(
            spot, spot, y_send.at[k, j], y_recv.at[k, j], (place(z, y_at(ROWS - j), core), x)
        )

    def c_copy(k, j):
        spot = qx.at[place(from_z(k), y_at(ROWS - j), core)]
        return remote(spot, spot, c_send.at[k, j], c_recv.at[k, j], (place(z, y, other), x))

    def c_arrival(k, j):
        spot = qx.at[place(from_z(k), y_at(ROWS - j), other)]
        return remote(spot, spot, c_send.at[k, j], c_recv.at[k, j], (place(z, y, other), x))

    def spread(k):
        for j in range(1, ROWS):
            y_copy(k, j).start()
        c_copy(k, 0).start()

    def handed(k):
        for j in range(1, ROWS):
            y_arrival(k, j).wait_recv()
            c_copy(k, j).start()

    @pl.loop(1, depth)
    def _(k):
        z_copy(k).start()

    spread(0)

    @pl.loop(0, steps)
    def _(step):
        w_copy(step).wait()
        span = pl.ds(pl.multiple_of(step * FORWARD, FORWARD), FORWARD)
        grown = jnp.maximum(dot(picked[...], w[:, span], NN) + bias[:, span], 1.0)
        product = grown[:count]
        for t in range(1, picks):
            product = product * grown[t * count : (t + 1) * count]
        rep[:, span] = jnp.log(product).astype(BF16)
        inv[:, span] = jnp.where(grown > 1.0, 1.0 / grown, 0.0).astype(BF16)

        @pl.when(step < depth - 1)
        def _():
            k = step + 1
            z_arrival(k).wait_recv()
            spread(k)
            handed(k - 1)

    wide = QUARTERS * count
    slot = me * count + lax.rem(iota((wide, docs_total), 0), count)
    lane = iota((wide, docs_total), 1)
    order = jnp.zeros((wide, docs_total), jnp.int32)
    for r in range(slots.shape[0]):
        order = order + jnp.where(slots[r : r + 1, :] == slot, lane + r * docs_total, 0)
    order = jnp.sum(order.astype(F32), axis=1, keepdims=True)
    upto = (iota((docs_total, docs_total), 0) <= iota((docs_total, docs_total), 1)).astype(F32).astype(BF16)
    amount = jnp.broadcast_to(counts[...].astype(F32), (8, docs_total))
    ends = dot(amount.astype(BF16), upto, NN)[:1]
    begins = ends - amount[:1]
    member = ((order >= begins) & (order < ends)).astype(F32).astype(BF16)
    diagonal = iota((wide, wide), 0) == iota((wide, wide), 1)
    weight_row = weights[...]
    weight_column = jnp.sum(jnp.where(diagonal, weight_row, 0.0), axis=1, keepdims=True)
    stacked = qx.shape[0] * qx.shape[1]
    per = qx.shape[1]
    each = per // QUARTERS
    one, two = iota((docs_total, stacked), 0), iota((docs_total, stacked), 1)
    select = (lax.div(one, each) == lax.div(two, per)) & (lax.rem(one, each) == lax.rem(two, each))
    select = select.astype(F32).astype(BF16)

    handed(depth - 1)

    @pl.loop(0, depth)
    def _(k):
        for j in range(ROWS):
            c_arrival(k, j).wait_recv()

    queries = qx[...].reshape(stacked, quarter)
    reps = jnp.concatenate([rep[:, i * quarter : (i + 1) * quarter] for i in range(QUARTERS)], axis=0)
    pair = dot(queries, reps, NT)
    row, column = iota((stacked, wide), 0), iota((stacked, wide), 1)
    pair = jnp.where(
        lax.rem(lax.div(row, each), QUARTERS) == lax.div(column, count), pair * weight_row, 0.0
    )
    high, low = halves(pair)
    paired = dot(select, high, NN) + dot(select, low, NN)
    high, low = halves(paired)
    parts[...] = dot(high, member, NN) + dot(low, member, NN)

    def group_peer(k):
        return (place(z, y, lax.rem(k, CORES)), lax.div(k, CORES))

    def rows_of(k):
        return pl.ds(pl.multiple_of(k * share, share), share)

    def a_copy(k):
        to = g_at(k)
        return remote(parts.at[rows_of(to)], box_a.at[g], a_send.at[k], a_recv.at[g], group_peer(to))

    def a_arrival(k):
        frm = g_at(k)
        return remote(box_a.at[frm], box_a.at[frm], a_send.at[k], a_recv.at[frm], group_peer(frm))

    for k in range(1, group):
        a_copy(k).start()
    box_a[g] = parts[rows_of(g), :]
    for k in range(1, group):
        a_arrival(k).wait_recv()
    box_b[y] = jnp.sum(box_a[...], axis=0)

    def b_copy(k):
        return remote(
            box_b.at[y], box_b.at[y], b_send.at[k], b_recv.at[y], (place(z, y_at(k), core), x)
        )

    def b_arrival(k):
        frm = y_at(k)
        return remote(
            box_b.at[frm], box_b.at[frm], b_send.at[k], b_recv.at[frm], (place(z, frm, core), x)
        )

    for k in range(1, ROWS):
        b_copy(k).start()
    for k in range(1, ROWS):
        b_arrival(k).wait_recv()
    box_c[z] = jnp.sum(box_b[...], axis=0)

    def d_copy(k):
        return remote(
            box_c.at[z], box_c.at[z], d_send.at[k], d_recv.at[z], (place(z_at(k), y, core), x)
        )

    def d_arrival(k):
        frm = z_at(k)
        return remote(
            box_c.at[frm], box_c.at[frm], d_send.at[k], d_recv.at[frm], (place(frm, y, core), x)
        )

    for k in range(1, depth):
        d_copy(k).start()
    for k in range(1, depth):
        d_arrival(k).wait_recv()
    scores[rows_of(g), :] = jnp.sum(box_c[...], axis=0)

    def e_copy(k):
        mine = scores.at[rows_of(g)]
        return remote(mine, mine, e_send.at[k], e_recv.at[g], group_peer(g_at(k)))

    def e_arrival(k):
        frm = g_at(k)
        theirs = scores.at[rows_of(frm)]
        return remote(theirs, theirs, e_send.at[k], e_recv.at[frm], group_peer(frm))

    for k in range(1, group):
        e_copy(k).start()
    for k in range(1, group):
        e_arrival(k).wait_recv()

    score = scores[...]
    shape = (docs_total, docs_total)
    owned = scores_out.shape[0]
    for r in range(owned):
        scores_out[r : r + 1, :] = jnp.sum(
            jnp.where(iota(shape, 0) == me * owned + r, score, 0.0), axis=0, keepdims=True
        )
    power = jnp.exp(score - jnp.max(score, axis=1, keepdims=True))
    prob = power / jnp.sum(power, axis=1, keepdims=True)
    dscore = (prob - (iota(shape, 0) == iota(shape, 1)).astype(F32)) / docs_total

    high, low = halves(dscore)
    per_query = (dot(member, high, NT) + dot(member, low, NT)) * weight_column
    high, low = halves(per_query)
    spread_out = dot(jnp.concatenate([high, low], axis=0), select, NN)
    row, column = iota((2 * wide, stacked), 0), iota((2 * wide, stacked), 1)
    keep = lax.rem(lax.div(row, count), QUARTERS) == lax.rem(lax.div(column, each), QUARTERS)
    spread_out = jnp.where(keep, spread_out, 0.0).astype(BF16)
    cut = 5 * 128

    @pl.loop(0, quarter // cut)
    def _(i):
        span = pl.ds(pl.multiple_of(i * cut, cut), cut)
        found = dot(spread_out, qx[:, :, span].reshape(stacked, cut), NN)
        found = found[:wide] + found[wide:]
        for part in range(QUARTERS):
            there = pl.ds(pl.multiple_of(part * quarter + i * cut, 128), cut)
            value = found[part * count : (part + 1) * count]
            for t in range(picks):
                lines = slice(t * count, (t + 1) * count)
                inv[lines, there] = (inv[lines, there].astype(F32) * value).astype(BF16)

    def block_rows(k):
        return pl.ds(pl.multiple_of(k * piece_rows, piece_rows), piece_rows)

    def x_peer(k):
        return (me, k)

    def r_copy(j, k):
        to = x_at(k)
        return remote(
            part_send.at[j, block_rows(to)],
            part_box.at[j, x],
            r_send.at[j, k],
            r_recv.at[j, x],
            x_peer(to),
        )

    def r_arrival(j, k):
        frm = x_at(k)
        spot = part_box.at[j, frm]
        return remote(spot, spot, r_send.at[j, k], r_recv.at[j, frm], x_peer(frm))

    def t_copy(j, k):
        mine = total.at[j, block_rows(x)]
        return remote(mine, mine, g_send.at[j, k], g_recv.at[j, x], x_peer(x_at(k)))

    def t_arrival(j, k):
        frm = x_at(k)
        theirs = total.at[j, block_rows(frm)]
        return remote(theirs, theirs, g_send.at[j, k], g_recv.at[j, frm], x_peer(frm))

    def finish(j):
        value = part_own[j, block_rows(x), :]
        for k in range(1, blocks):
            r_arrival(j, k).wait_recv()
            value = value + part_box[j, x_at(k)].astype(F32)
        total[j, block_rows(x), :] = value.astype(BF16)
        for k in range(1, blocks):
            t_copy(j, k).start()

    @pl.loop(0, 3)
    def _(j):
        span = pl.ds(pl.multiple_of(j * columns, columns), columns)
        value = dot(inv[...], w[span, :], NT)
        part_own[j] = value
        part_send[j] = value.astype(BF16)
        for k in range(1, blocks):
            r_copy(j, k).start()

        @pl.when(j >= 1)
        def _():
            finish(j - 1)

    finish(2)

    for j in range(3):
        for k in range(1, blocks):
            t_arrival(j, k).wait_recv()
        grad_out[:, j * columns : (j + 1) * columns] = dot(onehot[...], total[j], NN).astype(BF16)

    @pl.loop(1, depth)
    def _(k):
        z_copy(k).wait_send()

    @pl.loop(0, depth)
    def _(k):
        for j in range(ROWS):
            if j:
                y_copy(k, j).wait_send()
            c_copy(k, j).wait_send()

    for k in range(1, group):
        a_copy(k).wait_send()
        e_copy(k).wait_send()
    for k in range(1, ROWS):
        b_copy(k).wait_send()
    for k in range(1, depth):
        d_copy(k).wait_send()
    for j in range(3):
        for k in range(1, blocks):
            r_copy(j, k).wait_send()
            t_copy(j, k).wait_send()


def solution(mesh):
    passes, blocks = mesh.shape["pass"], mesh.shape["voc"]
    depth = passes // (ROWS * CORES)
    group = blocks * CORES

    def on_device(
        hidden, positions, passage_weight, passage_counts, passage_slot, head_weight, head_bias, queries
    ):
        count, length, width = hidden.shape
        picks = positions.shape[1]
        tokens = count * picks
        docs = passage_counts.shape[0]
        vocab = head_weight.shape[1]
        owned = queries.shape[0]
        quarter = vocab // QUARTERS
        per = QUARTERS * owned
        share = docs // group
        columns = width // 3
        target = (positions + length * jnp.arange(count, dtype=jnp.int32)[:, None]).T.reshape(1, tokens)
        piece = queries.reshape(owned, QUARTERS, quarter).transpose(1, 0, 2).reshape(per, quarter)
        vmem = pl.BlockSpec(memory_space=pltpu.VMEM)
        dma = pltpu.SemaphoreType.DMA
        scores, grad = pl.pallas_call(
            functools.partial(kernel, depth, blocks),
            out_shape=(
                jax.ShapeDtypeStruct((owned, docs), F32),
                jax.ShapeDtypeStruct((count * length, width), BF16),
            ),
            in_specs=[vmem, vmem, vmem, vmem, vmem, pl.BlockSpec(memory_space=pl.ANY), vmem, vmem],
            out_specs=(vmem, vmem),
            scratch_shapes=[
                pltpu.VMEM((width, vocab), BF16),
                pltpu.VMEM((tokens, vocab), BF16),
                pltpu.VMEM((count, vocab), BF16),
                pltpu.VMEM((8, 128), F32),
                pltpu.VMEM((passes, per, quarter), BF16),
                pltpu.VMEM((tokens, width), BF16),
                pltpu.VMEM((count * length, tokens), BF16),
                pltpu.VMEM((docs, docs), F32),
                pltpu.VMEM((group, share, docs), F32),
                pltpu.VMEM((ROWS, share, docs), F32),
                pltpu.VMEM((depth, share, docs), F32),
                pltpu.VMEM((docs, docs), F32),
                pltpu.VMEM((3, tokens, columns), F32),
                pltpu.VMEM((3, tokens, columns), BF16),
                pltpu.VMEM((3, blocks, tokens // blocks, columns), BF16),
                pltpu.VMEM((3, tokens, columns), BF16),
                dma((vocab // FORWARD,)),
                dma,
                dma((depth,)),
                dma((depth,)),
                dma((depth, ROWS)),
                dma((depth, ROWS)),
                dma((depth, ROWS)),
                dma((depth, ROWS)),
                dma((group,)),
                dma((group,)),
                dma((ROWS,)),
                dma((ROWS,)),
                dma((depth,)),
                dma((depth,)),
                dma((group,)),
                dma((group,)),
                dma((3, blocks)),
                dma((3, blocks)),
                dma((3, blocks)),
                dma((3, blocks)),
            ],
            compiler_params=pltpu.CompilerParams(collective_id=0, has_side_effects=True),
        )(
            hidden.reshape(count * length, width),
            target,
            jnp.tile(passage_weight, QUARTERS).reshape(1, QUARTERS * count),
            passage_counts.reshape(1, docs),
            passage_slot.reshape(-1, docs),
            head_weight,
            (head_bias + 1.0).reshape(1, vocab),
            piece,
        )
        return scores, grad.reshape(count, length, width)

    placed = (
        P("pass", None, None),
        P("pass", None),
        P("pass"),
        P(),
        P(),
        P(None, "voc"),
        P("voc"),
        P("pass", "voc"),
    )
    return jax.shard_map(
        on_device,
        mesh=mesh,
        in_specs=placed,
        out_specs=(P("pass", None), P("pass", None, None)),
        check_vma=False,
    )
```

time: 152 us -> 81.3 us (0.53)
  Pallas kernels: 0 us -> 71.2 us
  waiting for transfers between devices: 62.5 us -> 0 us
  matrix products: 30.7 us -> 0 us
  starting transfers between devices: 27.7 us -> 0 us
  blocking collectives: 15.3 us -> 0 us
  local copies, waits for them, and re-layouts: 12.7 us -> 7.22 us
    pallas_call x0 -> x1, Pallas kernels: none -> 71.2 us  [on_device(): pl.pallas_call(functools.partial(kernel, depth, blocks), out_shape=(jax.S...]
    all_to_all x4 -> x0, waiting for transfers between devices: 62.5 us -> none  [the longest x3 52.4 us: sent_to_all(): lax.all_to_all(jnp.broadcast_to(array[None], (size, *array.shape)), axis,...]
    dot_general x7 -> x0, matrix products: 30.7 us -> none  [the longest x1 14.1 us: on_device(): jnp.dot(picked, head_weight, preferred_element_type=jnp.float32) + head_bias]
    all_to_all x4 -> x0, starting transfers between devices: 27.7 us -> none  [the longest x3 20.9 us: sent_to_all(): lax.all_to_all(jnp.broadcast_to(array[None], (size, *array.shape)), axis,...]
    all_to_all x1 -> x0, blocking collectives: 15.3 us -> none  [sent_to_all(): lax.all_to_all(jnp.broadcast_to(array[None], (size, *array.shape)), axis,...]
    broadcast_in_dim x4 -> x0, local copies, waits for them, and re-layouts: 4.99 us -> none  [sent_to_all(): jnp.broadcast_to(array[None], (size, *array.shape))]
    unnamed x13 -> x2, local copies, waits for them, and re-layouts: 0.11 us -> 3.29 us
    gather x3 -> x0, local copies, waits for them, and re-layouts: 2.59 us -> none  [on_device(): picked = jax.vmap(lambda h, p: h[p])(hidden, positions).reshape(-1, width)]
  transfers between devices with their start and end apart: 4 -> 0, of which waited for: 4 -> 0; matrix products, arithmetic and copies ran while one was open for 13% -> 0% of each run, Pallas kernels for 0% -> 0%
where the time goes in v1:
time: 81.3 us; the launch traced here: 80.5 us
  Pallas kernels  71.2 us (88%)
  local copies, waits for them, and re-layouts  7.22 us (9%)
  other arithmetic  1.45 us (2%)
    pallas_call x1, Pallas kernels, on_device(): pl.pallas_call(functools.partial(kernel, depth, blocks), out_shape=(jax.S...  71.2 us
    unnamed x2, local copies, waits for them, and re-layouts  3.29 us

profile of v1, /device:TPU:1, one launch (start us, length us, event | category | flops | bytes accessed | tf_op | source)
XLA Modules:
  0.0 80.5 jit_solution(18261585422410991008)
XLA Ops:
  0.6 0.7 tile.2
  1.3 0.6 reshape_tile.3.weights
  1.9 0.7 add_bitcast_fusion
  2.6 0.6 reshape.35.target
  3.2 1.4 %reshape.40.q_own = bf16[8,1920]{1,0:T(8,128)(2,1)} reshape(bf16[4,2,1920]{2,1,0:T(2,128)(2,1)} %bitcast.11) | data formatting | bytes 61440 | tf_op jit(solution)/shard_map/reshape | solution.py:468
  4.6 0.8 broadcast_add_fusion
  5.4 0.6 reshape.38.bias
  6.0 71.2 %shard_map.95 = (f32[2,128]{1,0:T(2,128)}, bf16[512,768]{1,0:T(8,128)(2,1)}) custom-call(bf16[512,768]{1,0:T(8,128)(2,1)} %bitcast.9, s32[1,256]{1,0:T(1,128)} %reshape.35.target, f32[1,128]{1,0:T(1,128)} %reshape_tile.3.weights, s32[1,128]{1,0:T(1,128)} %bitcast.13, s32[16,128]{1,0:T(8,128)} %bitcast.12, bf16[768,7680]{1,0:T(8,128)(2,1)} %w_hbm.1, ...), custom_call_target="tpu_custom_call" | custom-call | tf_op jit(solution)/shard_map/pallas_call | solution.py:471
  77.2 1.2 %copy.13 = f32[2,128]{1,0:T(2,128)} copy(f32[2,128]{1,0:T(2,128)} %get-tuple-element.8) | data formatting | bytes 2048
  78.5 2.1 %copy.14 = bf16[32,16,768]{2,1,0:T(8,128)(2,1)} copy(bf16[32,16,768]{2,1,0:T(8,128)(2,1)} %bitcast.10) | data formatting | bytes 1572864
  (1 shorter events, 0.0 us)

commit v2 on v1

--- a/solution.py
+++ b/solution.py
@@ -12,6 +12,9 @@
 ROWS = 4
 QUARTERS = 4
 FORWARD = 512
+LAG = 3
+AWAY = (1, 3)
+HALF = (pl.ds(0, 1024), pl.ds(1024, 896))
 F32 = jnp.float32
 BF16 = jnp.bfloat16
 NT = (((1,), (1,)), ((), ()))
@@ -32,26 +35,45 @@
     return lax.broadcasted_iota(jnp.int32, shape, dim)
 
 
+def token_hits(positions, rows):
+    picks, count = positions.shape
+    tokens = picks * count
+    passage = (iota((count, tokens), 0) == lax.rem(iota((count, tokens), 1), count)).astype(F32)
+    spread = dot(positions[...].astype(F32).astype(BF16), passage.astype(BF16), NN)
+    own = iota((picks, tokens), 0) == lax.div(iota((picks, tokens), 1), count)
+    chosen = jnp.sum(jnp.where(own, spread, 0.0), axis=0, keepdims=True).astype(jnp.int32)
+    length = rows // count
+    goal = chosen + length * lax.rem(iota((1, tokens), 1), count)
+    return (iota((rows, tokens), 0) == goal).astype(F32).astype(BF16)
+
+
+def expand(positions, sums, scores, grad_out, scores_out):
+    scores_out[...] = scores[...]
+    hits = token_hits(positions, grad_out.shape[0])
+    columns = sums.shape[2]
+    for j in range(sums.shape[0]):
+        grad_out[:, j * columns : (j + 1) * columns] = dot(hits, sums[j], NN).astype(BF16)
+
+
 def kernel(
     depth,
     blocks,
-    hidden,
-    target,
-    weights,
-    counts,
-    slots,
+    hidden_hbm,
+    positions_hbm,
+    weights_hbm,
+    counts_hbm,
+    slots_hbm,
     w_hbm,
-    bias,
-    q_own,
+    bias_hbm,
+    q_hbm,
     scores_out,
-    grad_out,
+    total,
     w,
     inv,
     rep,
-    drep,
+    piece,
     qx,
     picked,
-    onehot,
     parts,
     box_a,
     box_b,
@@ -60,13 +82,22 @@
     part_own,
     part_send,
     part_box,
-    total,
+    hidden,
+    positions,
+    weights,
+    counts,
+    slots,
+    bias,
+    q_own,
+    in_sem,
     w_sem,
     q_sem,
     z_send,
     z_recv,
     y_send,
     y_recv,
+    h_send,
+    h_recv,
     c_send,
     c_recv,
     a_send,
@@ -122,17 +153,6 @@
 
     other = 1 - core
 
-    def w_copy(step):
-        span = pl.ds(pl.multiple_of(step * FORWARD, FORWARD), FORWARD)
-        return pltpu.make_async_copy(w_hbm.at[:, span], w.at[:, span], w_sem.at[step])
-
-    q_copy = pltpu.make_async_copy(q_own, qx.at[me], q_sem)
-    q_copy.start()
-
-    @pl.loop(0, steps)
-    def _(step):
-        w_copy(step).start()
-
     barrier = pltpu.get_barrier_semaphore()
     peers = [(place(z_at(k), y, core), x) for k in range(1, depth)]
     peers += [(place(z, y_at(k), core), x) for k in range(1, ROWS)]
@@ -140,10 +160,39 @@
     for peer in peers:
         pl.semaphore_signal(barrier, inc=1, device_id=peer, device_id_type=MESH)
 
-    rows = hidden.shape[0]
-    hit = (iota((rows, tokens), 0) == target[...]).astype(F32).astype(BF16)
-    onehot[...] = hit
-    picked[...] = dot(hit, hidden[...], TN).astype(BF16)
+    small = [
+        pltpu.make_async_copy(src, dst, in_sem.at[i])
+        for i, (src, dst) in enumerate(
+            (
+                (q_hbm, q_own),
+                (positions_hbm, positions),
+                (hidden_hbm, hidden),
+                (weights_hbm, weights),
+                (counts_hbm, counts),
+                (slots_hbm, slots),
+                (bias_hbm, bias),
+            )
+        )
+    ]
+    for copy in small:
+        copy.start()
+
+    def w_copy(step):
+        span = pl.ds(pl.multiple_of(step * FORWARD, FORWARD), FORWARD)
+        return pltpu.make_async_copy(w_hbm.at[:, span], w.at[:, span], w_sem.at[step])
+
+    @pl.loop(0, steps)
+    def _(step):
+        w_copy(step).start()
+
+    small[0].wait()
+    piece[...] = jnp.concatenate([q_own[i] for i in range(QUARTERS)], axis=0)
+    q_copy = pltpu.make_async_copy(piece, qx.at[me], q_sem)
+    q_copy.start()
+
+    for copy in small[1:]:
+        copy.wait()
+    picked[...] = dot(token_hits(positions, hidden.shape[0]), hidden[...], TN).astype(BF16)
 
     q_copy.wait()
     pl.semaphore_wait(barrier, len(peers))
@@ -171,31 +220,45 @@
 
     def y_copy(k, j):
         spot = qx.at[place(from_z(k), y, core)]
-        return remote(spot, spot, y_send.at[k, j], y_recv.at[k, j], (place(z, y_at(j), core), x))
+        return remote(spot, spot, y_send.at[k, j], y_recv.at[k, j], (place(z, y_at(AWAY[j]), core), x))
 
     def y_arrival(k, j):
-        spot = qx.at[place(from_z(k), y_at(ROWS - j), core)]
-        return remote(
-            spot, spot, y_send.at[k, j], y_recv.at[k, j], (place(z, y_at(ROWS - j), core), x)
-        )
+        frm = y_at(ROWS - AWAY[j])
+        spot = qx.at[place(from_z(k), frm, core)]
+        return remote(spot, spot, y_send.at[k, j], y_recv.at[k, j], (place(z, frm, core), x))
+
+    def h_copy(k, j):
+        spot = qx.at[place(from_z(k), y_at(ROWS - AWAY[j]), core), :, HALF[j]]
+        return remote(spot, spot, h_send.at[k, j], h_recv.at[k, j], (place(z, y_at(AWAY[j]), core), x))
+
+    def h_arrival(k, j):
+        spot = qx.at[place(from_z(k), y_at(2), core), :, HALF[j]]
+        frm = y_at(ROWS - AWAY[j])
+        return remote(spot, spot, h_send.at[k, j], h_recv.at[k, j], (place(z, frm, core), x))
 
     def c_copy(k, j):
-        spot = qx.at[place(from_z(k), y_at(ROWS - j), core)]
+        spot = qx.at[place(from_z(k), y_at(j), core)]
         return remote(spot, spot, c_send.at[k, j], c_recv.at[k, j], (place(z, y, other), x))
 
     def c_arrival(k, j):
-        spot = qx.at[place(from_z(k), y_at(ROWS - j), other)]
+        spot = qx.at[place(from_z(k), y_at(j), other)]
         return remote(spot, spot, c_send.at[k, j], c_recv.at[k, j], (place(z, y, other), x))
 
     def spread(k):
-        for j in range(1, ROWS):
+        for j in range(2):
             y_copy(k, j).start()
         c_copy(k, 0).start()
 
     def handed(k):
-        for j in range(1, ROWS):
+        for j in range(2):
             y_arrival(k, j).wait_recv()
-            c_copy(k, j).start()
+            h_copy(k, j).start()
+            c_copy(k, ROWS - AWAY[j]).start()
+
+    def relayed(k):
+        for j in range(2):
+            h_arrival(k, j).wait_recv()
+        c_copy(k, 2).start()
 
     @pl.loop(1, depth)
     def _(k):
@@ -207,7 +270,9 @@
     def _(step):
         w_copy(step).wait()
         span = pl.ds(pl.multiple_of(step * FORWARD, FORWARD), FORWARD)
-        grown = jnp.maximum(dot(picked[...], w[:, span], NN) + bias[:, span], 1.0)
+        lines = FORWARD // 128
+        offset = jnp.concatenate([bias[pl.ds(step * lines + i, 1), :] for i in range(lines)], axis=1) + 1.0
+        grown = jnp.maximum(dot(picked[...], w[:, span], NN) + offset, 1.0)
         product = grown[:count]
         for t in range(1, picks):
             product = product * grown[t * count : (t + 1) * count]
@@ -216,10 +281,16 @@
 
         @pl.when(step < depth - 1)
         def _():
-            k = step + 1
-            z_arrival(k).wait_recv()
-            spread(k)
-            handed(k - 1)
+            z_arrival(step + 1).wait_recv()
+            spread(step + 1)
+
+        @pl.when((step >= LAG) & (step < depth + LAG))
+        def _():
+            handed(step - LAG)
+
+        @pl.when((step >= 2 * LAG) & (step < depth + 2 * LAG))
+        def _():
+            relayed(step - 2 * LAG)
 
     wide = QUARTERS * count
     slot = me * count + lax.rem(iota((wide, docs_total), 0), count)
@@ -233,9 +304,11 @@
     ends = dot(amount.astype(BF16), upto, NN)[:1]
     begins = ends - amount[:1]
     member = ((order >= begins) & (order < ends)).astype(F32).astype(BF16)
+    diagonal = iota((count, count), 0) == iota((count, count), 1)
+    weight_column = jnp.sum(jnp.where(diagonal, weights[...], 0.0), axis=1, keepdims=True)
+    weight_column = jnp.concatenate([weight_column] * QUARTERS, axis=0)
     diagonal = iota((wide, wide), 0) == iota((wide, wide), 1)
-    weight_row = weights[...]
-    weight_column = jnp.sum(jnp.where(diagonal, weight_row, 0.0), axis=1, keepdims=True)
+    weight_row = jnp.sum(jnp.where(diagonal, weight_column, 0.0), axis=0, keepdims=True)
     stacked = qx.shape[0] * qx.shape[1]
     per = qx.shape[1]
     each = per // QUARTERS
@@ -243,7 +316,8 @@
     select = (lax.div(one, each) == lax.div(two, per)) & (lax.rem(one, each) == lax.rem(two, each))
     select = select.astype(F32).astype(BF16)
 
-    handed(depth - 1)
+    for k in range(steps - 2 * LAG, depth):
+        relayed(k)
 
     @pl.loop(0, depth)
     def _(k):
@@ -420,7 +494,6 @@
     for j in range(3):
         for k in range(1, blocks):
             t_arrival(j, k).wait_recv()
-        grad_out[:, j * columns : (j + 1) * columns] = dot(onehot[...], total[j], NN).astype(BF16)
 
     @pl.loop(1, depth)
     def _(k):
@@ -428,9 +501,10 @@
 
     @pl.loop(0, depth)
     def _(k):
+        for j in range(2):
+            y_copy(k, j).wait_send()
+            h_copy(k, j).wait_send()
         for j in range(ROWS):
-            if j:
-                y_copy(k, j).wait_send()
             c_copy(k, j).wait_send()
 
     for k in range(1, group):
@@ -464,26 +538,25 @@
         per = QUARTERS * owned
         share = docs // group
         columns = width // 3
-        target = (positions + length * jnp.arange(count, dtype=jnp.int32)[:, None]).T.reshape(1, tokens)
-        piece = queries.reshape(owned, QUARTERS, quarter).transpose(1, 0, 2).reshape(per, quarter)
+        piece = queries.reshape(owned, QUARTERS, quarter).transpose(1, 0, 2)
         vmem = pl.BlockSpec(memory_space=pltpu.VMEM)
+        anywhere = pl.BlockSpec(memory_space=pl.ANY)
         dma = pltpu.SemaphoreType.DMA
-        scores, grad = pl.pallas_call(
+        scores, sums = pl.pallas_call(
             functools.partial(kernel, depth, blocks),
             out_shape=(
                 jax.ShapeDtypeStruct((owned, docs), F32),
-                jax.ShapeDtypeStruct((count * length, width), BF16),
+                jax.ShapeDtypeStruct((3, tokens, columns), BF16),
             ),
-            in_specs=[vmem, vmem, vmem, vmem, vmem, pl.BlockSpec(memory_space=pl.ANY), vmem, vmem],
+            in_specs=[anywhere] * 8,
             out_specs=(vmem, vmem),
             scratch_shapes=[
                 pltpu.VMEM((width, vocab), BF16),
                 pltpu.VMEM((tokens, vocab), BF16),
                 pltpu.VMEM((count, vocab), BF16),
-                pltpu.VMEM((8, 128), F32),
+                pltpu.VMEM((per, quarter), BF16),
                 pltpu.VMEM((passes, per, quarter), BF16),
                 pltpu.VMEM((tokens, width), BF16),
-                pltpu.VMEM((count * length, tokens), BF16),
                 pltpu.VMEM((docs, docs), F32),
                 pltpu.VMEM((group, share, docs), F32),
                 pltpu.VMEM((ROWS, share, docs), F32),
@@ -492,13 +565,22 @@
                 pltpu.VMEM((3, tokens, columns), F32),
                 pltpu.VMEM((3, tokens, columns), BF16),
                 pltpu.VMEM((3, blocks, tokens // blocks, columns), BF16),
-                pltpu.VMEM((3, tokens, columns), BF16),
+                pltpu.VMEM((count * length, width), BF16),
+                pltpu.VMEM((picks, count), jnp.int32),
+                pltpu.VMEM((1, count), F32),
+                pltpu.VMEM((1, docs), jnp.int32),
+                pltpu.VMEM((passage_slot.shape[0] // docs, docs), jnp.int32),
+                pltpu.VMEM((vocab // 128, 128), F32),
+                pltpu.VMEM((QUARTERS, owned, quarter), BF16),
+                dma((7,)),
                 dma((vocab // FORWARD,)),
                 dma,
                 dma((depth,)),
                 dma((depth,)),
-                dma((depth, ROWS)),
-                dma((depth, ROWS)),
+                dma((depth, 2)),
+                dma((depth, 2)),
+                dma((depth, 2)),
+                dma((depth, 2)),
                 dma((depth, ROWS)),
                 dma((depth, ROWS)),
                 dma((group,)),
@@ -517,14 +599,23 @@
             compiler_params=pltpu.CompilerParams(collective_id=0, has_side_effects=True),
         )(
             hidden.reshape(count * length, width),
-            target,
-            jnp.tile(passage_weight, QUARTERS).reshape(1, QUARTERS * count),
+            positions.T,
+            passage_weight.reshape(1, count),
             passage_counts.reshape(1, docs),
             passage_slot.reshape(-1, docs),
             head_weight,
-            (head_bias + 1.0).reshape(1, vocab),
+            head_bias.reshape(vocab // 128, 128),
             piece,
         )
+        grad, scores = pl.pallas_call(
+            expand,
+            out_shape=(
+                jax.ShapeDtypeStruct((count * length, width), BF16),
+                jax.ShapeDtypeStruct((owned, docs), F32),
+            ),
+            in_specs=[vmem] * 3,
+            out_specs=(vmem, vmem),
+        )(positions.T, sums, scores)
         return scores, grad.reshape(count, length, width)
 
     placed = (

time: 81.3 us -> 67.8 us (0.83)
  local copies, waits for them, and re-layouts: 7.22 us -> 0 us
  Pallas kernels: 71.2 us -> 66.2 us
  other arithmetic: 1.45 us -> 0 us
    pallas_call x1, Pallas kernels: 71.2 us -> 63.8 us  [on_device(): pl.pallas_call(functools.partial(kernel, depth, blocks), out_shape=(jax.S...]
    unnamed x2 -> x0, local copies, waits for them, and re-layouts: 3.29 us -> none
    reshape x3 -> x0, local copies, waits for them, and re-layouts: 2.65 us -> none  [the longest x1 1.38 us: on_device(): queries.reshape(owned, QUARTERS, quarter).transpose(1, 0, 2)]
    pallas_call x0 -> x1, Pallas kernels: none -> 2.36 us  [on_device(): pl.pallas_call(expand, out_shape=(jax.ShapeDtypeStruct((count * length, w...]
    another operation x2 -> x0, local copies, waits for them, and re-layouts: 1.28 us -> none  [on_device(): jnp.tile(passage_weight, QUARTERS).reshape(1, QUARTERS * count)]
where the time goes in v2:
time: 67.8 us; the launch traced here: 66.8 us
  Pallas kernels  66.2 us (98%)
    pallas_call x1, Pallas kernels, on_device(): pl.pallas_call(functools.partial(kernel, depth, blocks), out_shape=(jax.S...  63.8 us
    pallas_call x1, Pallas kernels, on_device(): pl.pallas_call(expand, out_shape=(jax.ShapeDtypeStruct((count * length, w...  2.36 us

profile of v2, /device:TPU:1, one launch (start us, length us, event | category | flops | bytes accessed | tf_op | source)
XLA Modules:
  0.0 66.8 jit_solution(10751406097374590916)
XLA Ops:
  0.6 63.8 %shard_map.95 = (f32[2,128]{1,0:T(2,128)}, bf16[3,256,256]{2,1,0:T(8,128)(2,1)}) custom-call(bf16[512,768]{1,0:T(8,128)(2,1)} %bitcast.10, s32[8,32]{1,0:T(8,128)} %bitcast.13, f32[1,32]{1,0:T(1,128)} %bitcast.16, s32[1,128]{1,0:T(1,128)} %bitcast.17, s32[16,128]{1,0:T(8,128)} %bitcast.15, bf16[768,7680]{1,0:T(8,128)(2,1)} %w_hbm.1, f32[60,128]{1,0:T(8,128)} %bitcast.11, ...), custom_call_target="tpu_custom_call" | custom-call | tf_op jit(solution)/shard_map/pallas_call | solution.py:545
  64.4 2.4 %shard_map.96 = (bf16[512,768]{1,0:T(8,128)(2,1)}, f32[2,128]{1,0:T(2,128)}) custom-call(s32[8,32]{1,0:T(8,128)} %bitcast.14, bf16[3,256,256]{2,1,0:T(8,128)(2,1)} %get-tuple-element.6.sums, f32[2,128]{1,0:T(2,128)} %get-tuple-element.7.scores), custom_call_target="tpu_custom_call" | custom-call | tf_op jit(solution)/shard_map/pallas_call | solution.py:610

commit v3 on v2

--- a/solution.py
+++ b/solution.py
@@ -47,12 +47,20 @@
     return (iota((rows, tokens), 0) == goal).astype(F32).astype(BF16)
 
 
-def expand(positions, sums, scores, grad_out, scores_out):
+def expand(hits, sums, scores, grad_hbm, scores_out, grad, out_sem):
     scores_out[...] = scores[...]
-    hits = token_hits(positions, grad_out.shape[0])
+    pieces, rows, _ = grad.shape
     columns = sums.shape[2]
-    for j in range(sums.shape[0]):
-        grad_out[:, j * columns : (j + 1) * columns] = dot(hits, sums[j], NN).astype(BF16)
+    stores = []
+    for i in range(pieces):
+        lines = slice(i * rows, (i + 1) * rows)
+        for j in range(sums.shape[0]):
+            grad[i, :, j * columns : (j + 1) * columns] = dot(hits[lines, :], sums[j], NN).astype(BF16)
+        store = pltpu.make_async_copy(grad.at[i], grad_hbm.at[pl.ds(i * rows, rows)], out_sem.at[i])
+        store.start()
+        stores.append(store)
+    for store in stores:
+        store.wait()
 
 
 def kernel(
@@ -68,6 +76,7 @@
     q_hbm,
     scores_out,
     total,
+    hits,
     w,
     inv,
     rep,
@@ -130,6 +139,7 @@
     steps = vocab // FORWARD
     columns = width // 3
     tokens = picked.shape[0]
+    lots = part_own.shape[0]
     piece_rows = tokens // blocks
 
     def place(zz, yy, cc):
@@ -192,7 +202,9 @@
 
     for copy in small[1:]:
         copy.wait()
-    picked[...] = dot(token_hits(positions, hidden.shape[0]), hidden[...], TN).astype(BF16)
+    hit = token_hits(positions, hidden.shape[0])
+    hits[...] = hit
+    picked[...] = dot(hit, hidden[...], TN).astype(BF16)
 
     q_copy.wait()
     pl.semaphore_wait(barrier, len(peers))
@@ -432,10 +444,10 @@
         found = found[:wide] + found[wide:]
         for part in range(QUARTERS):
             there = pl.ds(pl.multiple_of(part * quarter + i * cut, 128), cut)
-            value = found[part * count : (part + 1) * count]
+            value = found[part * count : (part + 1) * count].astype(BF16)
             for t in range(picks):
                 lines = slice(t * count, (t + 1) * count)
-                inv[lines, there] = (inv[lines, there].astype(F32) * value).astype(BF16)
+                inv[lines, there] = inv[lines, there] * value
 
     def block_rows(k):
         return pl.ds(pl.multiple_of(k * piece_rows, piece_rows), piece_rows)
@@ -476,7 +488,7 @@
         for k in range(1, blocks):
             t_copy(j, k).start()
 
-    @pl.loop(0, 3)
+    @pl.loop(0, lots)
     def _(j):
         span = pl.ds(pl.multiple_of(j * columns, columns), columns)
         value = dot(inv[...], w[span, :], NT)
@@ -485,13 +497,11 @@
         for k in range(1, blocks):
             r_copy(j, k).start()
 
-        @pl.when(j >= 1)
-        def _():
-            finish(j - 1)
-
-    finish(2)
-
-    for j in range(3):
+    for j in range(lots):
+        finish(j)
+
+    @pl.loop(0, lots)
+    def _(j):
         for k in range(1, blocks):
             t_arrival(j, k).wait_recv()
 
@@ -514,7 +524,9 @@
         b_copy(k).wait_send()
     for k in range(1, depth):
         d_copy(k).wait_send()
-    for j in range(3):
+
+    @pl.loop(0, lots)
+    def _(j):
         for k in range(1, blocks):
             r_copy(j, k).wait_send()
             t_copy(j, k).wait_send()
@@ -538,18 +550,20 @@
         per = QUARTERS * owned
         share = docs // group
         columns = width // 3
+        lots = 3
         piece = queries.reshape(owned, QUARTERS, quarter).transpose(1, 0, 2)
         vmem = pl.BlockSpec(memory_space=pltpu.VMEM)
         anywhere = pl.BlockSpec(memory_space=pl.ANY)
         dma = pltpu.SemaphoreType.DMA
-        scores, sums = pl.pallas_call(
+        scores, sums, hits = pl.pallas_call(
             functools.partial(kernel, depth, blocks),
             out_shape=(
-                jax.ShapeDtypeStruct((owned, docs), F32),
-                jax.ShapeDtypeStruct((3, tokens, columns), BF16),
+                pltpu.VMEM((owned, docs), F32),
+                pltpu.VMEM((lots, tokens, columns), BF16),
+                pltpu.VMEM((count * length, tokens), BF16),
             ),
             in_specs=[anywhere] * 8,
-            out_specs=(vmem, vmem),
+            out_specs=(vmem, vmem, vmem),
             scratch_shapes=[
                 pltpu.VMEM((width, vocab), BF16),
                 pltpu.VMEM((tokens, vocab), BF16),
@@ -562,9 +576,9 @@
                 pltpu.VMEM((ROWS, share, docs), F32),
                 pltpu.VMEM((depth, share, docs), F32),
                 pltpu.VMEM((docs, docs), F32),
-                pltpu.VMEM((3, tokens, columns), F32),
-                pltpu.VMEM((3, tokens, columns), BF16),
-                pltpu.VMEM((3, blocks, tokens // blocks, columns), BF16),
+                pltpu.VMEM((lots, tokens, columns), F32),
+                pltpu.VMEM((lots, tokens, columns), BF16),
+                pltpu.VMEM((lots, blocks, tokens // blocks, columns), BF16),
                 pltpu.VMEM((count * length, width), BF16),
                 pltpu.VMEM((picks, count), jnp.int32),
                 pltpu.VMEM((1, count), F32),
@@ -591,10 +605,10 @@
                 dma((depth,)),
                 dma((group,)),
                 dma((group,)),
-                dma((3, blocks)),
-                dma((3, blocks)),
-                dma((3, blocks)),
-                dma((3, blocks)),
+                dma((lots, blocks)),
+                dma((lots, blocks)),
+                dma((lots, blocks)),
+                dma((lots, blocks)),
             ],
             compiler_params=pltpu.CompilerParams(collective_id=0, has_side_effects=True),
         )(
@@ -614,8 +628,9 @@
                 jax.ShapeDtypeStruct((owned, docs), F32),
             ),
             in_specs=[vmem] * 3,
-            out_specs=(vmem, vmem),
-        )(positions.T, sums, scores)
+            out_specs=(anywhere, vmem),
+            scratch_shapes=[pltpu.VMEM((4, count * length // 4, width), BF16), dma((4,))],
+        )(*(pltpu.with_memory_space_constraint(kept, pltpu.VMEM) for kept in (hits, sums, scores)))
         return scores, grad.reshape(count, length, width)
 
     placed = (

time: 67.8 us -> 64.6 us (0.953); the launches traced: 66.8 us -> 64.6 us
  Pallas kernels: 66.2 us -> 63.9 us
    pallas_call x1, Pallas kernels: 63.8 us -> 62.2 us  [on_device(): pl.pallas_call(functools.partial(kernel, depth, blocks), out_shape=(pltpu...]
where the time goes in v3:
time: 64.6 us
  Pallas kernels  63.9 us (99%)
    pallas_call x1, Pallas kernels, on_device(): pl.pallas_call(functools.partial(kernel, depth, blocks), out_shape=(pltpu...  62.2 us
    pallas_call x1, Pallas kernels, on_device(): pl.pallas_call(expand, out_shape=(jax.ShapeDtypeStruct((count * length, w...  1.71 us

profile of v3, /device:TPU:1, one launch (start us, length us, event | category | flops | bytes accessed | tf_op | source)
XLA Modules:
  0.0 64.6 jit_solution(13784645552191879390)
XLA Ops:
  0.6 62.2 %shard_map.95 = (f32[2,128]{1,0:T(2,128)S(1)}, bf16[3,256,256]{2,1,0:T(8,128)(2,1)S(1)}, bf16[512,256]{1,0:T(8,128)(2,1)S(1)}) custom-call(bf16[512,768]{1,0:T(8,128)(2,1)} %bitcast.10, s32[8,32]{1,0:T(8,128)} %bitcast.14, f32[1,32]{1,0:T(1,128)} %bitcast.15, s32[1,128]{1,0:T(1,128)} %bitcast.16, s32[16,128]{1,0:T(8,128)} %bitcast.13, ...), custom_call_target="tpu_custom_call" | custom-call | tf_op jit(solution)/shard_map/pallas_call | solution.py:558
  62.8 1.7 %shard_map.96 = (bf16[512,768]{1,0:T(8,128)(2,1)}, f32[2,128]{1,0:T(2,128)}) custom-call(bf16[512,256]{1,0:T(8,128)(2,1)S(1)} %get-tuple-element.7.hits, bf16[3,256,256]{2,1,0:T(8,128)(2,1)S(1)} %get-tuple-element.8.sums, f32[2,128]{1,0:T(2,128)S(1)} %get-tuple-element.9.scores), custom_call_target="tpu_custom_call" | custom-call | tf_op jit(solution)/shard_map/pallas_call | solution.py:624

commit v4 on v3

--- a/solution.py
+++ b/solution.py
@@ -12,7 +12,7 @@
 ROWS = 4
 QUARTERS = 4
 FORWARD = 512
-LAG = 3
+LAG = 7
 AWAY = (1, 3)
 HALF = (pl.ds(0, 1024), pl.ds(1024, 896))
 F32 = jnp.float32
@@ -200,12 +200,6 @@
     q_copy = pltpu.make_async_copy(piece, qx.at[me], q_sem)
     q_copy.start()
 
-    for copy in small[1:]:
-        copy.wait()
-    hit = token_hits(positions, hidden.shape[0])
-    hits[...] = hit
-    picked[...] = dot(hit, hidden[...], TN).astype(BF16)
-
     q_copy.wait()
     pl.semaphore_wait(barrier, len(peers))
 
@@ -277,6 +271,12 @@
         z_copy(k).start()
 
     spread(0)
+
+    for copy in small[1:]:
+        copy.wait()
+    hit = token_hits(positions, hidden.shape[0])
+    hits[...] = hit
+    picked[...] = dot(hit, hidden[...], TN).astype(BF16)
 
     @pl.loop(0, steps)
     def _(step):

time: 64.6 us -> 62.5 us (0.967)
  Pallas kernels: 63.9 us -> 61.7 us
    pallas_call x1, Pallas kernels: 62.2 us -> 60 us  [on_device(): pl.pallas_call(functools.partial(kernel, depth, blocks), out_shape=(pltpu...]
where the time goes in v4:
time: 62.5 us; the launch traced here: 62.4 us
  Pallas kernels  61.7 us (99%)
  between operations  0.64 us (1%)
    pallas_call x1, Pallas kernels, on_device(): pl.pallas_call(functools.partial(kernel, depth, blocks), out_shape=(pltpu...  60 us
    pallas_call x1, Pallas kernels, on_device(): pl.pallas_call(expand, out_shape=(jax.ShapeDtypeStruct((count * length, w...  1.71 us

profile of v4, /device:TPU:1, one launch (start us, length us, event | category | flops | bytes accessed | tf_op | source)
XLA Modules:
  0.0 62.4 jit_solution(13519781808531104641)
XLA Ops:
  0.6 60.0 %shard_map.95 = (f32[2,128]{1,0:T(2,128)S(1)}, bf16[3,256,256]{2,1,0:T(8,128)(2,1)S(1)}, bf16[512,256]{1,0:T(8,128)(2,1)S(1)}) custom-call(bf16[512,768]{1,0:T(8,128)(2,1)} %bitcast.10, s32[8,32]{1,0:T(8,128)} %bitcast.14, f32[1,32]{1,0:T(1,128)} %bitcast.15, s32[1,128]{1,0:T(1,128)} %bitcast.16, s32[16,128]{1,0:T(8,128)} %bitcast.13, ...), custom_call_target="tpu_custom_call" | custom-call | tf_op jit(solution)/shard_map/pallas_call | solution.py:558
  60.7 1.7 %shard_map.96 = (bf16[512,768]{1,0:T(8,128)(2,1)}, f32[2,128]{1,0:T(2,128)}) custom-call(bf16[512,256]{1,0:T(8,128)(2,1)S(1)} %get-tuple-element.7.hits, bf16[3,256,256]{2,1,0:T(8,128)(2,1)S(1)} %get-tuple-element.8.sums, f32[2,128]{1,0:T(2,128)S(1)} %get-tuple-element.9.scores), custom_call_target="tpu_custom_call" | custom-call | tf_op jit(solution)/shard_map/pallas_call | solution.py:624

commit v5 on v4

--- a/solution.py
+++ b/solution.py
@@ -13,7 +13,8 @@
 QUARTERS = 4
 FORWARD = 512
 LAG = 7
-AWAY = (1, 3)
+AWAY = (1, 3, 2)
+FAR = 4
 HALF = (pl.ds(0, 1024), pl.ds(1024, 896))
 F32 = jnp.float32
 BF16 = jnp.bfloat16
@@ -253,24 +254,40 @@
     def spread(k):
         for j in range(2):
             y_copy(k, j).start()
+
+        @pl.when(k >= FAR)
+        def _():
+            y_copy(k, 2).start()
+
         c_copy(k, 0).start()
 
     def handed(k):
         for j in range(2):
             y_arrival(k, j).wait_recv()
-            h_copy(k, j).start()
+
+            @pl.when(k < FAR)
+            def _():
+                h_copy(k, j).start()
+
             c_copy(k, ROWS - AWAY[j]).start()
 
     def relayed(k):
-        for j in range(2):
-            h_arrival(k, j).wait_recv()
+        @pl.when(k < FAR)
+        def _():
+            for j in range(2):
+                h_arrival(k, j).wait_recv()
+
+        @pl.when(k >= FAR)
+        def _():
+            y_arrival(k, 2).wait_recv()
+
         c_copy(k, 2).start()
 
     @pl.loop(1, depth)
     def _(k):
         z_copy(k).start()
 
-    spread(0)
+    spread(jnp.int32(0))
 
     for copy in small[1:]:
         copy.wait()
@@ -328,7 +345,8 @@
     select = (lax.div(one, each) == lax.div(two, per)) & (lax.rem(one, each) == lax.rem(two, each))
     select = select.astype(F32).astype(BF16)
 
-    for k in range(steps - 2 * LAG, depth):
+    @pl.loop(steps - 2 * LAG, depth)
+    def _(k):
         relayed(k)
 
     @pl.loop(0, depth)
@@ -365,6 +383,27 @@
     for k in range(1, group):
         a_copy(k).start()
     box_a[g] = parts[rows_of(g), :]
+
+    @pl.loop(1, depth)
+    def _(k):
+        z_copy(k).wait_send()
+
+    @pl.loop(0, depth)
+    def _(k):
+        for j in range(2):
+            y_copy(k, j).wait_send()
+
+            @pl.when(k < FAR)
+            def _():
+                h_copy(k, j).wait_send()
+
+        @pl.when(k >= FAR)
+        def _():
+            y_copy(k, 2).wait_send()
+
+        for j in range(ROWS):
+            c_copy(k, j).wait_send()
+
     for k in range(1, group):
         a_arrival(k).wait_recv()
     box_b[y] = jnp.sum(box_a[...], axis=0)
@@ -504,18 +543,6 @@
     def _(j):
         for k in range(1, blocks):
             t_arrival(j, k).wait_recv()
-
-    @pl.loop(1, depth)
-    def _(k):
-        z_copy(k).wait_send()
-
-    @pl.loop(0, depth)
-    def _(k):
-        for j in range(2):
-            y_copy(k, j).wait_send()
-            h_copy(k, j).wait_send()
-        for j in range(ROWS):
-            c_copy(k, j).wait_send()
 
     for k in range(1, group):
         a_copy(k).wait_send()
@@ -591,8 +618,8 @@
                 dma,
                 dma((depth,)),
                 dma((depth,)),
-                dma((depth, 2)),
-                dma((depth, 2)),
+                dma((depth, 3)),
+                dma((depth, 3)),
                 dma((depth, 2)),
                 dma((depth, 2)),
                 dma((depth, ROWS)),

time: 62.5 us -> 61.2 us (0.979)
  Pallas kernels: 61.7 us -> 60.5 us
    pallas_call x1, Pallas kernels: 60 us -> 58.8 us  [on_device(): pl.pallas_call(functools.partial(kernel, depth, blocks), out_shape=(pltpu...]
where the time goes in v5:
time: 61.2 us; the launch traced here: 61.1 us
  Pallas kernels  60.5 us (99%)
  between operations  0.64 us (1%)
    pallas_call x1, Pallas kernels, on_device(): pl.pallas_call(functools.partial(kernel, depth, blocks), out_shape=(pltpu...  58.8 us
    pallas_call x1, Pallas kernels, on_device(): pl.pallas_call(expand, out_shape=(jax.ShapeDtypeStruct((count * length, w...  1.71 us

profile of v5, /device:TPU:1, one launch (start us, length us, event | category | flops | bytes accessed | tf_op | source)
XLA Modules:
  0.0 61.1 jit_solution(15065981899354313386)
XLA Ops:
  0.6 58.8 %shard_map.95 = (f32[2,128]{1,0:T(2,128)S(1)}, bf16[3,256,256]{2,1,0:T(8,128)(2,1)S(1)}, bf16[512,256]{1,0:T(8,128)(2,1)S(1)}) custom-call(bf16[512,768]{1,0:T(8,128)(2,1)} %bitcast.10, s32[8,32]{1,0:T(8,128)} %bitcast.14, f32[1,32]{1,0:T(1,128)} %bitcast.15, s32[1,128]{1,0:T(1,128)} %bitcast.16, s32[16,128]{1,0:T(8,128)} %bitcast.13, ...), custom_call_target="tpu_custom_call" | custom-call | tf_op jit(solution)/shard_map/pallas_call | solution.py:585
  59.4 1.7 %shard_map.96 = (bf16[512,768]{1,0:T(8,128)(2,1)}, f32[2,128]{1,0:T(2,128)}) custom-call(bf16[512,256]{1,0:T(8,128)(2,1)S(1)} %get-tuple-element.7.hits, bf16[3,256,256]{2,1,0:T(8,128)(2,1)S(1)} %get-tuple-element.8.sums, f32[2,128]{1,0:T(2,128)S(1)} %get-tuple-element.9.scores), custom_call_target="tpu_custom_call" | custom-call | tf_op jit(solution)/shard_map/pallas_call | solution.py:651

commit v6 on v5

--- a/solution.py
+++ b/solution.py
@@ -14,7 +14,7 @@
 FORWARD = 512
 LAG = 7
 AWAY = (1, 3, 2)
-FAR = 4
+FAR = 0
 HALF = (pl.ds(0, 1024), pl.ds(1024, 896))
 F32 = jnp.float32
 BF16 = jnp.bfloat16

time: 61.2 us -> 61.3 us (level)
  no operation moved by 1% of the time
where the time goes in v6:
time: 61.3 us; the launch traced here: 61.2 us
  Pallas kernels  60.6 us (99%)
  between operations  0.64 us (1%)
    pallas_call x1, Pallas kernels, on_device(): pl.pallas_call(functools.partial(kernel, depth, blocks), out_shape=(pltpu...  58.9 us
    pallas_call x1, Pallas kernels, on_device(): pl.pallas_call(expand, out_shape=(jax.ShapeDtypeStruct((count * length, w...  1.71 us

profile of v6, /device:TPU:1, one launch (start us, length us, event | category | flops | bytes accessed | tf_op | source)
XLA Modules:
  0.0 61.2 jit_solution(6759392937999183035)
XLA Ops:
  0.6 58.9 %shard_map.95 = (f32[2,128]{1,0:T(2,128)S(1)}, bf16[3,256,256]{2,1,0:T(8,128)(2,1)S(1)}, bf16[512,256]{1,0:T(8,128)(2,1)S(1)}) custom-call(bf16[512,768]{1,0:T(8,128)(2,1)} %bitcast.10, s32[8,32]{1,0:T(8,128)} %bitcast.14, f32[1,32]{1,0:T(1,128)} %bitcast.15, s32[1,128]{1,0:T(1,128)} %bitcast.16, s32[16,128]{1,0:T(8,128)} %bitcast.13, ...), custom_call_target="tpu_custom_call" | custom-call | tf_op jit(solution)/shard_map/pallas_call | solution.py:585
  59.5 1.7 %shard_map.96 = (bf16[512,768]{1,0:T(8,128)(2,1)}, f32[2,128]{1,0:T(2,128)}) custom-call(bf16[512,256]{1,0:T(8,128)(2,1)S(1)} %get-tuple-element.7.hits, bf16[3,256,256]{2,1,0:T(8,128)(2,1)S(1)} %get-tuple-element.8.sums, f32[2,128]{1,0:T(2,128)S(1)} %get-tuple-element.9.scores), custom_call_target="tpu_custom_call" | custom-call | tf_op jit(solution)/shard_map/pallas_call | solution.py:651
